TPU v7x, 512 devices: a whole 4x4x16 slice. The times are simulated.
512 devices in a mesh: subj: 32 (over y, z_lo), slab: 16 (over x, z_hi, core).
Axes of the slice: x: 4, y: 4, z: 16 (z_hi: 2, z_lo: 8; z = z_hi * 8 + z_lo), core: 2. Of those that a mesh axis runs over, the one named last changes fastest.
Arguments:
- image: float32 [32, 192, 32, 192], P('subj', 'slab'), may hold values from -6 to 6
- velocity: float32 [32, 3, 192, 32, 192], P('subj', None, 'slab'), may hold values from -3 to 3
- template: float32 [192, 32, 192], P('slab', 'subj'), may hold values from -6 to 6
- z_kernel: float32 [192, 192], replicated, as said below
- x_kernel: float32 [192, 192], replicated, as said below
Outputs:
- velocity_update: float32 [32, 3, 192, 32, 192], P('subj', None, 'slab')
- new_template: float32 [192, 32, 192], P('slab', 'subj')
Inputs may be any that keep to these rules, and one draw needn't show every extreme that they name: `z_kernel`: entries are positive. `x_kernel`: entries are positive.
All inputs are finite; a program needn't handle non-finite values.
Results may differ from a plain program's by a relative error of at most 0.00028.
Values sent between devices are 32-bit elements; how exact they have to be, the bound alone decides.
No kernel may reach another device: no remote copies, remote signals or barrier semaphores. Data moves between devices by JAX's collectives and lax.ppermute only.
A program may use at most 64 MiB of HBM per device.

v0:
```python
import jax
import jax.numpy as jnp
from jax import lax
from jax.sharding import PartitionSpec as P


def with_halo(x, sides, width):
    for axis, dim in sides:
        size, length = (lax.axis_size(axis), x.shape[dim])
        up = [(i, (i + 1) % size) for i in range(size - 1)]
        down = [(j, i) for i, j in up]
        last = lax.slice_in_dim(x, length - width, length, axis=dim)
        leading = lax.slice_in_dim(x, 0, width, axis=dim)
        before = lax.ppermute(last, axis, up)
        after = lax.ppermute(leading, axis, down)
        x = jnp.concatenate([before, x, after], axis=dim)
    return x


def gradients(padded):
    slope_z = (padded[2:, 1:-1, 1:-1] - padded[:-2, 1:-1, 1:-1]) * 0.5
    slope_y = (padded[1:-1, 2:, 1:-1] - padded[1:-1, :-2, 1:-1]) * 0.5
    slope_x = (padded[1:-1, 1:-1, 2:] - padded[1:-1, 1:-1, :-2]) * 0.5
    return jnp.stack([slope_z, slope_y, slope_x])


def per_device(image, velocity, template, z_kernel, x_kernel):
    highest = lax.Precision.HIGHEST
    full_rows = lax.all_gather(template, "subj", axis=1, tiled=True)
    with_rims = with_halo(full_rows, (("slab", 0),), 1)
    padded = jnp.pad(with_rims, ((0, 0), (1, 1), (1, 1)))
    slopes = gradients(padded)
    warped = full_rows[None] + jnp.sum(velocity * slopes[None], 1)
    residual = image - warped
    forces = residual[:, None] * slopes[None]
    along_x = jnp.einsum("sczyx,wx->sczyw", forces, x_kernel, precision=highest)
    along_z = jnp.einsum(
        "vz,sczyx->scvyx",
        z_kernel,
        lax.all_to_all(along_x, "slab", split_axis=3, concat_axis=2, tiled=True),
        precision=highest,
    )
    velocity_update = lax.all_to_all(along_z, "slab", split_axis=2, concat_axis=3, tiled=True)
    local_sum = jnp.sum(residual, 0)
    subjects = lax.axis_size("subj") * image.shape[0]
    summed = lax.psum_scatter(local_sum, "subj", scatter_dimension=1, tiled=True)
    new_template = template + summed / subjects
    return (velocity_update, new_template)


def solution(mesh):
    in_specs = (
        P("subj", "slab", None, None),
        P("subj", None, "slab", None, None),
        P("slab", "subj", None),
        P(),
        P(),
    )
    out_specs = (P("subj", None, "slab", None, None), P("slab", "subj", None))
    return jax.shard_map(
        per_device, mesh=mesh, in_specs=in_specs, out_specs=out_specs, check_vma=False
    )
```

profile of v0, /device:TPU:4, one launch (start us, length us, event | category | flops | bytes accessed | tf_op | source)
XLA Modules:
  0.0 502.2 jit_solution(7305345701270509311)
XLA Ops:
  7.2 0.0 copy-start
  7.2 0.8 copy.43
  7.9 130.0 %all_gather.3 = f32[12,32,192]{2,0,1:T(8,128)S(1)} all-gather(f32[12,1,192]{2,0,1:T(8,128)S(1)} %copy.43), channel_id=1, replica_groups=mesh['subj'=32,'slab'=16] {'subj'}, dimensions={1}, use_global_device_ids=true | all-gather | bytes 304128 | tf_op jit(solution)/shard_map/all_gather | solution.py:29
  138.0 1.9 collective-permute-start.1
  139.9 13.3 %collective-permute-start = (f32[1,32,192]{2,0,1:T(1,128)S(1)}, f32[1,32,192]{2,0,1:T(1,128)S(1)}, u32[]{:S(2)}, u32[]{:S(2)}) collective-permute-start(f32[1,32,192]{2,0,1:T(1,128)S(1)} %get-tuple-element.13), channel_id=1, source_target_pairs={{1,0},{2,1},{3,2},{4,3},{5,4},{6,5},{7,6},{8,7},{9,8},{10,9},{11,1... | collective-permute-start | bytes 73736 | tf_op jit(solution)/shard_map/ppermute | solution.py:15
  153.1 0.0 collective-permute-done.1
  153.2 1.6 collective-permute-done
  154.7 0.3 select_maximum_fusion
  155.1 0.0 copy-start.2
  155.1 0.6 fusion.10
  155.7 0.6 copy-done.2
  156.3 0.0 copy-start.3
  156.3 1.0 fusion
  157.4 0.0 copy-done.3
  157.4 0.3 fusion.14
  157.7 0.0 copy-start.1
  157.7 0.2 fusion.3
  158.0 0.5 copy-done.1
  158.5 0.0 copy-done
  158.5 1.7 convolution_bitcast_fusion.1
  160.2 1.2 copy.47
  161.4 70.8 %all_to_all.33 = f32[1,3,12,32,192]{4,0,2,1,3:T(1,128)S(1)} all-to-all(f32[1,3,12,32,192]{4,0,2,1,3:T(1,128)S(1)} %copy.47), channel_id=1, replica_groups=mesh['subj'=32,'slab'=16] {'slab'}, dimensions={3} | all-to-all | bytes 1769472 | tf_op jit(solution)/shard_map/all_to_all | solution.py:40
  232.3 1.3 copy.48
  233.6 0.0 copy-start.4
  233.6 0.6 copy.49
  234.2 0.3 copy-done.4
  234.5 2.3 convolution_bitcast_fusion
  236.8 1.5 copy.51
  238.4 0.0 copy-start.5
  238.4 8.6 %all-to-all-start.1 = ((f32[1,3,192,2,192]{4,3,1,0,2:T(2,128)}), f32[1,3,192,2,192]{4,3,1,0,2:T(2,128)S(1)}, u32[]{:S(2)}, u32[]{:S(2)}) async-start(f32[1,3,192,2,192]{4,3,1,0,2:T(2,128)} %copy.51), calls=%async_computation.1 | async-start | bytes 2359296 | tf_op jit(solution)/shard_map/all_to_all | solution.py:43
  246.9 0.0 reduce-scatter.2.cloned.1.call-start
  247.0 0.7 reduce-scatter.2.cloned.1.call-update
  247.6 243.6 %reduce-scatter.2.cloned.1.call-done = f32[12,1,192]{2,0,1:T(8,128)} async-done(((f32[12,32,192]{2,0,1:T(8,128)}), f32[12,1,192]{2,0,1:T(8,128)}) %reduce-scatter.2.cloned.1.call-update) | async-done | bytes 9232 | tf_op jit(solution)/shard_map/reduce_scatter | solution.py:46
  491.3 0.0 copy-done.5
  491.3 0.7 multiply_add_fusion
  492.0 0.6 copy.56
  492.6 0.0 all-to-all-done.1
  492.6 0.4 copy.52
  493.0 1.2 copy.53
  494.2 1.1 copy.55
  (1 shorter events, 0.0 us)
Async XLA Ops:
  7.2 151.3 %copy-start = (f32[192,192]{1,0:T(8,128)S(1)}, f32[192,192]{1,0:T(8,128)}, u32[]{:S(2)}) copy-start(f32[192,192]{1,0:T(8,128)} %param.9) | copy-start | bytes 442372
  138.0 15.2 %collective-permute-start.1 = (f32[1,32,192]{2,0,1:T(1,128)S(1)}, f32[1,32,192]{2,0,1:T(1,128)S(1)}, u32[]{:S(2)}, u32[]{:S(2)}) collective-permute-start(f32[1,32,192]{2,0,1:T(1,128)S(1)} %get-tuple-element.12), channel_id=1, source_target_pairs={{0,1},{1,2},{2,3},{3,4},{4,5},{5,6},{6,7},{7,8},{8,9},{9,10},{10,1... | collective-permute-start | bytes 73736 | tf_op jit(solution)/shard_map/ppermute | solution.py:14
  139.9 14.8 %collective-permute-start = (f32[1,32,192]{2,0,1:T(1,128)S(1)}, f32[1,32,192]{2,0,1:T(1,128)S(1)}, u32[]{:S(2)}, u32[]{:S(2)}) collective-permute-start(f32[1,32,192]{2,0,1:T(1,128)S(1)} %get-tuple-element.13), channel_id=1, source_target_pairs={{1,0},{2,1},{3,2},{4,3},{5,4},{6,5},{7,6},{8,7},{9,8},{10,9},{11,1... | collective-permute-start | bytes 73736 | tf_op jit(solution)/shard_map/ppermute | solution.py:15
  155.1 1.3 copy-start.2
  156.3 1.1 copy-start.3
  157.7 0.8 copy-start.1
  233.6 0.9 copy-start.4
  238.4 252.9 %copy-start.5 = (f32[12,1,192]{2,1,0:T(1,128)S(1)}, f32[12,1,192]{2,1,0:T(1,128)}, u32[]{:S(2)}) copy-start(f32[12,1,192]{2,1,0:T(1,128)} %param.7) | copy-start | bytes 27652
  238.4 254.3 %all-to-all-start.1 = ((f32[1,3,192,2,192]{4,3,1,0,2:T(2,128)}), f32[1,3,192,2,192]{4,3,1,0,2:T(2,128)S(1)}, u32[]{:S(2)}, u32[]{:S(2)}) async-start(f32[1,3,192,2,192]{4,3,1,0,2:T(2,128)} %copy.51), calls=%async_computation.1 | async-start | bytes 2359296 | tf_op jit(solution)/shard_map/all_to_all | solution.py:43
  246.9 244.4 %reduce-scatter.2.cloned.1.call-start = ((), (), s32[]{:S(2)}) async-start(), calls=%async_computation.3 | async-start | bytes 540672 | tf_op jit(solution)/shard_map/reduce_scatter | solution.py:46
Sparse Core Ops, SparseCore 0:
  250.5 240.7 reduce-scatter.1
where the time goes:
time: 503 us; the launch traced here: 502 us
  waiting for transfers between devices  246 us (49%)
  blocking collectives  201 us (40%)
  starting transfers between devices  23.8 us (5%)
  between operations  14.2 us (3%)
  local copies, waits for them, and re-layouts  10.3 us (2%)
    reduce_scatter x1, waiting for transfers between devices, per_device(): lax.psum_scatter(local_sum, 'subj', scatter_dimension=1, tiled=True)  244 us
    all_gather x1, blocking collectives, per_device(): full_rows = lax.all_gather(template, 'subj', axis=1, tiled=True)  130 us
    all_to_all x1, blocking collectives, per_device(): lax.all_to_all(along_x, 'slab', split_axis=3, concat_axis=2, tiled=True)  70.8 us
    ppermute x1, starting transfers between devices, with_halo(): after = lax.ppermute(leading, axis, down)  13.3 us
  transfers between devices with their start and end apart: 4, of which 2 were waited for; matrix products, arithmetic and copies ran while one was open for 0% of the time, Pallas kernels for 0%

commit v1 on v0

--- a/solution.py
+++ b/solution.py
@@ -26,7 +26,12 @@
 
 def per_device(image, velocity, template, z_kernel, x_kernel):
     highest = lax.Precision.HIGHEST
-    full_rows = lax.all_gather(template, "subj", axis=1, tiled=True)
+    full_rows = jnp.concatenate(
+        lax.all_to_all(
+            jnp.stack([template] * lax.axis_size("subj")), "subj", concat_axis=0, split_axis=0
+        ),
+        axis=1,
+    )
     with_rims = with_halo(full_rows, (("slab", 0),), 1)
     padded = jnp.pad(with_rims, ((0, 0), (1, 1), (1, 1)))
     slopes = gradients(padded)

time: 503 us -> 422 us (0.84)
  blocking collectives: 201 us -> 106 us
  waiting for transfers between devices: 246 us -> 259 us
    all_gather x1 -> x0, blocking collectives: 130 us -> none  [per_device(): full_rows = lax.all_gather(template, 'subj', axis=1, tiled=True)]
    all_to_all x0 -> x1, blocking collectives: none -> 40.2 us  [per_device(): lax.all_to_all(jnp.stack([template] * lax.axis_size('subj')), 'subj', con...]
    reduce_scatter x1, waiting for transfers between devices: 244 us -> 257 us  [per_device(): lax.psum_scatter(local_sum, 'subj', scatter_dimension=1, tiled=True)]
  transfers between devices with their start and end apart: 4 -> 4, of which waited for: 2 -> 2; matrix products, arithmetic and copies ran while one was open for 0% -> 1% of each run, Pallas kernels for 0% -> 0%
where the time goes in v1:
time: 422 us; the launch traced here: 421 us
  waiting for transfers between devices  259 us (61%)
  blocking collectives  106 us (25%)
  starting transfers between devices  24.6 us (6%)
  between operations  14.2 us (3%)
  local copies, waits for them, and re-layouts  12 us (3%)
    reduce_scatter x1, waiting for transfers between devices, per_device(): lax.psum_scatter(local_sum, 'subj', scatter_dimension=1, tiled=True)  257 us
    all_to_all x1, blocking collectives, per_device(): lax.all_to_all(along_x, 'slab', split_axis=3, concat_axis=2, tiled=True)  66.2 us
    all_to_all x1, blocking collectives, per_device(): lax.all_to_all(jnp.stack([template] * lax.axis_size('subj')), 'subj', con...  40.2 us
    ppermute x1, starting transfers between devices, with_halo(): after = lax.ppermute(leading, axis, down)  13.3 us
    all_to_all x1, starting transfers between devices, per_device(): lax.all_to_all(along_z, 'slab', split_axis=2, concat_axis=3, tiled=True)  9.39 us
  transfers between devices with their start and end apart: 4, of which 2 were waited for; matrix products, arithmetic and copies ran while one was open for 1% of the time, Pallas kernels for 0%

profile of v1, /device:TPU:4, one launch (start us, length us, event | category | flops | bytes accessed | tf_op | source)
XLA Modules:
  0.0 421.4 jit_solution(9024128651024589568)
XLA Ops:
  7.2 0.0 copy-start
  7.2 0.8 copy.64
  7.9 0.2 stack.10
  8.1 40.2 %all_to_all.38 = f32[32,12,1,192]{3,2,1,0:T(1,128)S(1)} all-to-all(f32[32,12,1,192]{3,2,1,0:T(1,128)S(1)} %stack.10), channel_id=1, replica_groups=mesh['subj'=32,'slab'=16] {'subj'}, dimensions={0} | all-to-all | bytes 589824 | tf_op jit(solution)/shard_map/all_to_all | solution.py:30
  48.3 0.1 copy.63
  48.4 1.9 collective-permute-start.1
  50.4 13.3 %collective-permute-start = (f32[1,32,192]{2,1,0:T(8,128)S(1)}, f32[1,32,192]{2,1,0:T(8,128)S(1)}, u32[]{:S(2)}, u32[]{:S(2)}) collective-permute-start(f32[1,32,192]{2,1,0:T(8,128)S(1)} %get-tuple-element.13), channel_id=1, source_target_pairs={{1,0},{2,1},{3,2},{4,3},{5,4},{6,5},{7,6},{8,7},{9,8},{10,9},{11,1... | collective-permute-start | bytes 73736 | tf_op jit(solution)/shard_map/ppermute | solution.py:15
  63.6 0.0 collective-permute-done.1
  63.6 1.6 collective-permute-done
  65.2 0.2 select_maximum_fusion
  65.4 0.0 copy-start.1
  65.4 0.4 fusion.10
  65.8 0.9 copy-done.1
  66.7 0.0 copy-start.2
  66.7 0.3 fusion
  67.0 0.7 copy-done.2
  67.7 0.1 fusion.15
  67.8 0.0 copy-done
  67.8 1.1 convolution_bitcast_fusion.1
  69.0 1.2 copy.42
  70.2 66.2 %all_to_all.39 = f32[1,3,12,32,192]{4,0,2,1,3:T(1,128)S(1)} all-to-all(f32[1,3,12,32,192]{4,0,2,1,3:T(1,128)S(1)} %copy.42), channel_id=1, replica_groups=mesh['subj'=32,'slab'=16] {'slab'}, dimensions={3} | all-to-all | bytes 1769472 | tf_op jit(solution)/shard_map/all_to_all | solution.py:45
  136.4 1.3 copy.43
  137.7 0.0 copy-start.3
  137.7 0.6 copy.44
  138.4 0.3 copy-done.3
  138.7 2.3 convolution_bitcast_fusion
  141.0 1.5 copy.46
  142.5 9.4 %all-to-all-start.2 = ((f32[1,3,192,2,192]{4,3,1,0,2:T(2,128)}), f32[1,3,192,2,192]{4,3,1,0,2:T(2,128)S(1)}, u32[]{:S(2)}, u32[]{:S(2)}) async-start(f32[1,3,192,2,192]{4,3,1,0,2:T(2,128)} %copy.46), calls=%async_computation.2 | async-start | bytes 2359296 | tf_op jit(solution)/shard_map/all_to_all | solution.py:48
  151.9 0.0 copy-start.4
  151.9 0.0 reduce-scatter.2.cloned.1.call-start
  152.0 1.0 copy.49
  153.0 0.0 reduce-scatter.2.cloned.1.call-update
  153.0 257.5 %reduce-scatter.2.cloned.1.call-done = f32[12,1,192]{2,0,1:T(8,128)} async-done(((f32[12,32,192]{2,0,1:T(8,128)}), f32[12,1,192]{2,0,1:T(8,128)}) %reduce-scatter.2.cloned.1.call-update) | async-done | bytes 9232 | tf_op jit(solution)/shard_map/reduce_scatter | solution.py:51
  410.5 0.0 copy-done.4
  410.5 0.7 copy_add_fusion
  411.2 0.6 copy.52
  411.8 0.0 all-to-all-done.2
  411.8 0.4 copy.47
  412.2 1.2 copy.48
  413.4 1.1 copy.51
  (1 shorter events, 0.0 us)
Async XLA Ops:
  7.2 60.7 %copy-start = (f32[192,192]{1,0:T(8,128)S(1)}, f32[192,192]{1,0:T(8,128)}, u32[]{:S(2)}) copy-start(f32[192,192]{1,0:T(8,128)} %param.9) | copy-start | bytes 442372
  48.4 15.2 %collective-permute-start.1 = (f32[1,32,192]{2,1,0:T(8,128)S(1)}, f32[1,32,192]{2,1,0:T(8,128)S(1)}, u32[]{:S(2)}, u32[]{:S(2)}) collective-permute-start(f32[1,32,192]{2,1,0:T(8,128)S(1)} %get-tuple-element.12), channel_id=1, source_target_pairs={{0,1},{1,2},{2,3},{3,4},{4,5},{5,6},{6,7},{7,8},{8,9},{9,10},{10,1... | collective-permute-start | bytes 73736 | tf_op jit(solution)/shard_map/ppermute | solution.py:14
  50.4 14.8 %collective-permute-start = (f32[1,32,192]{2,1,0:T(8,128)S(1)}, f32[1,32,192]{2,1,0:T(8,128)S(1)}, u32[]{:S(2)}, u32[]{:S(2)}) collective-permute-start(f32[1,32,192]{2,1,0:T(8,128)S(1)} %get-tuple-element.13), channel_id=1, source_target_pairs={{1,0},{2,1},{3,2},{4,3},{5,4},{6,5},{7,6},{8,7},{9,8},{10,9},{11,1... | collective-permute-start | bytes 73736 | tf_op jit(solution)/shard_map/ppermute | solution.py:15
  65.4 1.3 copy-start.1
  66.7 1.0 copy-start.2
  137.7 0.9 copy-start.3
  142.5 269.3 %all-to-all-start.2 = ((f32[1,3,192,2,192]{4,3,1,0,2:T(2,128)}), f32[1,3,192,2,192]{4,3,1,0,2:T(2,128)S(1)}, u32[]{:S(2)}, u32[]{:S(2)}) async-start(f32[1,3,192,2,192]{4,3,1,0,2:T(2,128)} %copy.46), calls=%async_computation.2 | async-start | bytes 2359296 | tf_op jit(solution)/shard_map/all_to_all | solution.py:48
  151.9 258.6 %copy-start.4 = (f32[12,1,192]{2,1,0:T(1,128)S(1)}, f32[12,1,192]{2,1,0:T(1,128)}, u32[]{:S(2)}) copy-start(f32[12,1,192]{2,1,0:T(1,128)} %param.7) | copy-start | bytes 27652
  151.9 258.6 %reduce-scatter.2.cloned.1.call-start = ((), (), s32[]{:S(2)}) async-start(), calls=%async_computation.4 | async-start | bytes 540672 | tf_op jit(solution)/shard_map/reduce_scatter | solution.py:51
Sparse Core Ops, SparseCore 0:
  155.5 254.8 reduce-scatter.1
